TPU v7x, 256 devices: a whole 4x4x8 slice. The times are simulated.
256 devices in a mesh: row: 16 (over y, x_lo, core), col: 16 (over x_hi, z).
Axes of the slice: x: 4 (x_hi: 2, x_lo: 2; x = x_hi * 2 + x_lo), y: 4, z: 8, core: 2. Of those that a mesh axis runs over, the one named last changes fastest.
Arguments:
- amplitudes: float32 [32, 4, 512, 512], P('row', None, 'col'), may hold values from -6 to 6
- integrals: float32 [4, 512, 32, 512], P(None, 'row', 'col'), may hold values from -0.125 to 0.125
- occ_energy: float32 [32], replicated, may hold values from -1.5 to -0.3
- vir_energy: float32 [512], replicated, may hold values from 0.2 to 3
Outputs:
- update: float32 [32, 32, 512, 512], P('row', None, 'col')
All inputs are finite; a program needn't handle non-finite values.
Results may differ from a plain program's by a relative error of at most 0.00007.
Values sent between devices are 32-bit elements; how exact they have to be, the bound alone decides.
A program may use at most 64 MiB of HBM per device.

v0:
```python
import jax
import jax.numpy as jnp
from jax import lax
from jax.sharding import PartitionSpec as P


def body(amplitudes, integrals, occ_energy, vir_energy):
    moved = lax.all_to_all(amplitudes, "col", split_axis=3, concat_axis=2, tiled=True)
    panel = lax.all_gather(moved, "col", axis=3, tiled=True)
    rows_i = panel.shape[0]
    cycle = jnp.einsum(
        "ikac,kcjb->ijab",
        panel,
        lax.all_gather(integrals, "row", axis=1, tiled=True),
        precision=lax.Precision.HIGHEST,
    )
    back = lax.all_to_all(cycle, "col", split_axis=2, concat_axis=1, tiled=True)
    a_local = back.shape[2]
    occ_local = lax.dynamic_slice_in_dim(occ_energy, lax.axis_index("row") * rows_i, rows_i, 0)
    vir_local = lax.dynamic_slice_in_dim(vir_energy, lax.axis_index("col") * a_local, a_local, 0)
    denom = (
        occ_local[:, None, None, None]
        + occ_energy[None, :, None, None]
        - vir_local[None, None, :, None]
        - vir_energy[None, None, None, :]
    )
    return back / denom


def solution(mesh):
    return jax.shard_map(
        body,
        mesh=mesh,
        in_specs=(P("row", None, "col", None), P(None, "row", "col", None), P(), P()),
        out_specs=P("row", None, "col", None),
        check_vma=False,
    )
```

profile of v0, /device:TPU:1, one launch (start us, length us, event | category | flops | bytes accessed | tf_op | source)
XLA Modules:
  0.0 364.8 jit_solution(3342363447694086450)
XLA Ops:
  6.5 1.9 copy.15
  8.5 0.0 all-gather.3.cloned.1.call-update
  8.5 0.0 all-gather.5.cloned.1.call-start
  8.6 2.0 copy.16
  10.5 1.4 reshape.43
  11.9 26.7 %all_to_all.36 = f32[16,1,8192]{2,1,0:T(1,128)S(1)} all-to-all(f32[16,1,8192]{2,1,0:T(1,128)S(1)} %reshape.43), channel_id=1, replica_groups=mesh['row'=16,'col'=16] {'col'}, dimensions={0} | all-to-all | bytes 1048576 | tf_op jit(solution)/shard_map/all_to_all | solution.py:8
  38.6 0.5 broadcast.37
  39.1 1.9 reduce
  41.0 1.1 reshape.44
  42.1 2.5 copy.24
  44.6 3.0 all_to_all.29
  47.6 25.2 %all-gather.3.cloned.1.call-done = f32[4,512,2,512]{3,1,0,2:T(8,128)} async-done(((f32[4,32,2,512]{3,1,0,2:T(8,128)}), f32[4,512,2,512]{3,1,0,2:T(8,128)}) %all-gather.3.cloned.1.call-update) | async-done | bytes 8388624 | tf_op jit(solution)/shard_map/all_gather | solution.py:14
  72.8 137.5 %all-gather.5.cloned.1.call-done = f32[2,4,512,512]{2,3,1,0:T(8,128)} async-done(((f32[2,4,512,32]{2,3,1,0:T(8,128)}), f32[2,4,512,512]{2,3,1,0:T(8,128)}) %all-gather.5.cloned.1.call-update) | async-done | bytes 8388624 | tf_op jit(solution)/shard_map/all_gather | solution.py:9
  210.3 32.5 %fusion.3 = f32[2,2,512,512]{2,3,0,1:T(8,128)} fusion(f32[2,4,512,512]{2,3,1,0:T(8,128)} %all-gather.5.cloned.1.call-done, f32[4,512,2,512]{3,1,0,2:T(8,128)} %all-gather.3.cloned.1.call-done), kind=kOutput, calls=%fused_computation.4 | convolution fusion | flops 25769803776 | bytes 20971520 | tf_op jit(solution)/shard_map/ikac,kcjb->ijab/dot_general | solution.py:11
  242.8 7.3 %copy.18 = f32[2,2,512,512]{3,0,1,2:T(2,128)} copy(f32[2,2,512,512]{2,3,0,1:T(8,128)} %fusion.3) | data formatting | bytes 8388608 | tf_op jit(solution)/shard_map/ikac,kcjb->ijab/transpose | solution.py:11
  250.1 4.7 %all-to-all-start.1 = ((f32[2,2,512,512]{3,0,1,2:T(2,128)}), f32[2,2,512,512]{3,0,1,2:T(2,128)}, u32[]{:S(2)}, u32[]{:S(2)}) async-start(f32[2,2,512,512]{3,0,1,2:T(2,128)} %copy.18), calls=%async_computation.1 | async-start | bytes 8388608 | tf_op jit(solution)/shard_map/all_to_all | solution.py:17
  254.8 0.1 dynamic_slice.7
  254.9 0.1 dynamic_slice.6
  254.9 0.1 broadcast_add_fusion
  255.0 0.1 broadcast_subtract_fusion
  255.1 95.9 %all-to-all-done.1 = f32[2,2,512,512]{3,0,1,2:T(2,128)} async-done(((f32[2,2,512,512]{3,0,1,2:T(2,128)}), f32[2,2,512,512]{3,0,1,2:T(2,128)}, u32[]{:S(2)}, u32[]{:S(2)}) %all-to-all-start.1) | async-done | bytes 4194336 | tf_op jit(solution)/shard_map/all_to_all | solution.py:17
  351.0 3.5 copy.19
  354.5 0.8 copy.20
  355.4 2.6 subtract_divide_fusion
  (6 shorter events, 0.0 us)
Async XLA Ops:
  6.5 66.2 %all-gather.3.cloned.1.call-start = ((), (), s32[]{:S(2)}) async-start(), calls=%async_computation.2 | async-start | bytes 8912896 | tf_op jit(solution)/shard_map/all_gather | solution.py:14
  8.5 201.7 %all-gather.5.cloned.1.call-start = ((), (), s32[]{:S(2)}) async-start(), calls=%async_computation.3 | async-start | bytes 8912896 | tf_op jit(solution)/shard_map/all_gather | solution.py:9
  250.1 4.7 %copy-start = (f32[512]{0:T(512)S(1)}, f32[512]{0:T(512)}, u32[]{:S(2)}) copy-start(f32[512]{0:T(512)} %param.7) | copy-start | bytes 6148
  250.1 4.8 %copy-start.1 = (f32[32]{0:T(128)S(1)}, f32[32]{0:T(128)}, u32[]{:S(2)}) copy-start(f32[32]{0:T(128)} %param.6) | copy-start | bytes 388
  250.1 100.9 %all-to-all-start.1 = ((f32[2,2,512,512]{3,0,1,2:T(2,128)}), f32[2,2,512,512]{3,0,1,2:T(2,128)}, u32[]{:S(2)}, u32[]{:S(2)}) async-start(f32[2,2,512,512]{3,0,1,2:T(2,128)} %copy.18), calls=%async_computation.1 | async-start | bytes 8388608 | tf_op jit(solution)/shard_map/all_to_all | solution.py:17
Sparse Core Ops, SparseCore 0:
  9.1 63.5 all-gather.2
  75.4 134.8 all-gather.4
where the time goes:
time: 365 us
  waiting for transfers between devices  259 us (71%)
  matrix products  32.5 us (9%)
  blocking collectives  26.7 us (7%)
  local copies, waits for them, and re-layouts  24.2 us (7%)
  between operations  13.5 us (4%)
  starting transfers between devices  4.71 us (1%)
  other arithmetic  4.68 us (1%)
    all_gather x1, waiting for transfers between devices, body(): panel = lax.all_gather(moved, 'col', axis=3, tiled=True)  137 us
    all_to_all x1, waiting for transfers between devices, body(): back = lax.all_to_all(cycle, 'col', split_axis=2, concat_axis=1, tiled=True)  95.9 us
    dot_general x1, matrix products, body(): jnp.einsum('ikac,kcjb->ijab', panel, lax.all_gather(integrals, 'row', axi...  32.5 us
    all_to_all x1, blocking collectives, body(): lax.all_to_all(amplitudes, 'col', split_axis=3, concat_axis=2, tiled=True)  26.7 us
    all_gather x1, waiting for transfers between devices, body(): lax.all_gather(integrals, 'row', axis=1, tiled=True)  25.2 us
    transpose x1, local copies, waits for them, and re-layouts, body(): jnp.einsum('ikac,kcjb->ijab', panel, lax.all_gather(integrals, 'row', axi...  7.32 us
  transfers between devices with their start and end apart: 3, of which 3 were waited for; matrix products, arithmetic and copies ran while one was open for 3% of the time, Pallas kernels for 0%

commit v1 on v0

v1 whole, which is shorter than its diff:
```python
import jax
import jax.numpy as jnp
from jax import lax
from jax.experimental import pallas as pl
from jax.experimental.pallas import tpu as pltpu
from jax.sharding import PartitionSpec as P

MESH = pl.DeviceIdType.MESH
NZ = 8


def place(x, y, z, core):
    return (y * 4 + (x % 2) * 2 + core, (x // 2) * NZ + z)


def kernel(t_hbm, w_hbm, out, w_raw, w_src, w_buf, t_buf, t_hi, t_lo, acc,
           load_sem, pre_send, pre_recv, ring_send, ring_recv, part_send, part_recv,
           t_send, t_recv, c_send, c_recv, own_sem):
    row, col = lax.axis_index("row"), lax.axis_index("col")
    y, xl, core = row // 4, (row // 2) % 2, row % 2
    xh, z = col // NZ, col % NZ
    x = xh * 2 + xl
    par = y % 2
    s = y * 2 + xl
    y_pair = y + 1 - 2 * par

    def flip(v, bits, width):
        for b in range(width):
            if (bits >> b) & 1:
                v = v + (1 << b) * (1 - 2 * ((v // (1 << b)) % 2))
        return v

    def remote(src, dst, send, recv, device):
        return pltpu.make_async_remote_copy(src, dst, send, recv, device_id=device, device_id_type=MESH)

    pre_dev = {}
    for e in range(1, 8):
        se = flip(s, e, 3)
        pre_dev[e] = (se // 2, se % 2)
    group = [(dx, dp) for dx in (1, 3, 0, 2) for dp in (0, 1) if (dx, dp) != (0, 0)]
    z_next = {0: (z + 1) % NZ, 1: (z + NZ - 1) % NZ}
    partner = place(x, y, z, 1 - core)

    def group_dev(dx, dp):
        return place((x + dx) % 4, y_pair if dp else y, z, core)

    everyone = [place(xh * 2 + pre_dev[e][1], pre_dev[e][0], z, core) for e in pre_dev]
    everyone += [group_dev(dx, dp) for dx, dp in group]
    everyone += [place(x, y, z_next[0], core), place(x, y, z_next[1], core), partner]

    load_w = pltpu.make_async_copy(w_hbm, w_raw, load_sem.at[0])
    load_w.start()
    own_u = x * 2 + par
    load_t = pltpu.make_async_copy(t_hbm, t_buf.at[own_u], load_sem.at[1])
    load_t.start()

    barrier = pltpu.get_barrier_semaphore()
    for d in everyone:
        pl.semaphore_signal(barrier, inc=1, device_id=d, device_id_type=MESH)

    load_w.wait()
    for k in range(4):
        for jj in range(2):
            for bh in range(2):
                w_src[jj, bh, k] = w_raw[k, :, jj, bh * 256:bh * 256 + 256]
    pl.semaphore_wait(barrier, len(everyone))

    own_w = pltpu.make_async_copy(w_src.at[xl, par], w_buf.at[z, :, s, core], load_sem.at[2])
    own_w.start()
    pending = []

    def start(cp):
        cp.start()
        pending.append(cp)

    def pre(e):
        ye, xe = pre_dev[e]
        return remote(w_src.at[xe, ye % 2], w_buf.at[z, :, s, core], pre_send.at[e], pre_recv.at[e],
                      place(xh * 2 + xe, ye, z, core))

    def pre_wait(e):
        ye, xe = pre_dev[e]
        view = w_buf.at[z, :, ye * 2 + xe, core]
        remote(view, view, pre_send.at[e], pre_recv.at[e], partner).wait_recv()

    for e in (1, 2, 3, 6, 7, 4, 5):
        start(pre(e))

    xm, xp = (x + 3) % 4, (x + 1) % 4
    dev_y, dev_xp, dev_xm = group_dev(0, 1), group_dev(1, 0), group_dev(3, 0)

    def t_view(u, half):
        return t_buf.at[u] if half is None else t_buf.at[u, half]

    def t_copy(u, half, k, device, src=None):
        v = t_view(u, half)
        start(remote(v if src is None else src, v, t_send.at[k], t_recv.at[k], device))

    def t_wait(u, half, k):
        v = t_view(u, half)
        remote(v, v, t_send.at[k], t_recv.at[k], partner).wait_recv()

    t_copy(own_u, None, 0, dev_y, t_hbm)
    t_copy(own_u, None, 1, dev_xp, t_hbm)
    t_copy(own_u, None, 3, dev_xm, t_hbm)

    chunks = [(s, 1), (flip(s, 1, 3), 1), ((flip(s, 2, 3) // 2) * 2, 2), ((flip(s, 4, 3) // 4) * 4, 4)]
    fresh = {0: (), 1: (1,), 2: (2, 3), 3: (4, 5, 6, 7)}

    def w_view(zs, ch, which):
        base, size = chunks[ch]
        return w_buf.at[zs, :, pl.ds(base, size), which]

    def slice_at(d, n):
        return (z + NZ - n) % NZ if d == 0 else (z + n) % NZ

    def ring_wait(d, n, ch):
        v = w_view(slice_at(d, n), ch, core)
        remote(v, v, ring_send.at[d, n - 1, ch], ring_recv.at[d, n - 1, ch], partner).wait_recv()

    def ring_forward(d, n, ch):
        v = w_view(slice_at(d, n), ch, core)
        start(remote(v, v, ring_send.at[d, n, ch], ring_recv.at[d, n, ch], place(x, y, z_next[d], core)))

    def slot_of(d, n):
        return 0 if n == 0 else 7 if n == 4 else 2 * n - 1 + d

    def to_partner(d, n, ch):
        v = w_view(slice_at(d, n), ch, core)
        k = slot_of(d, n)
        start(remote(v, v, part_send.at[k, ch], part_recv.at[k, ch], partner))

    def partner_wait(d, n):
        k = slot_of(d, n)
        for ch in range(4):
            v = w_view(slice_at(d, n), ch, 1 - core)
            remote(v, v, part_send.at[k, ch], part_recv.at[k, ch], partner).wait_recv()

    def goes_on(d, n, ch):
        return n < 3 or (n == 3 and ((ch < 3) if d == 0 else (ch == 3)))

    def relay(n):
        for ch in range(4):
            if n == 0:
                for e in fresh[ch]:
                    pre_wait(e)
            for d in range(2):
                if n > 0:
                    ring_wait(d, n, ch)
                if goes_on(d, n, ch):
                    ring_forward(d, n, ch)
                if n > 0 or d == 0:
                    to_partner(d, n, ch)

    def convert(u):
        for i in range(2):
            for k in range(4):
                v = t_buf[u, i, k]
                hi = v.astype(jnp.bfloat16)
                rows = pl.ds(pl.multiple_of(u * 64 + i * 32, 32), 32)
                t_hi[k, rows, :] = hi
                t_lo[k, rows, :] = (v - hi.astype(jnp.float32)).astype(jnp.bfloat16)

    def compute(d, n):
        zs = slice_at(d, n)
        k_slot = slot_of(d, n)

        def step(k, carry):
            w = w_buf[zs, k].reshape(512, 256)
            w_hi = w.astype(jnp.bfloat16)
            w_lo = (w - w_hi.astype(jnp.float32)).astype(jnp.bfloat16)
            p = jnp.dot(t_hi[k], w_hi, preferred_element_type=jnp.float32)
            p += jnp.dot(t_lo[k], w_hi, preferred_element_type=jnp.float32)
            p += jnp.dot(t_hi[k], w_lo, preferred_element_type=jnp.float32)
            p = p.reshape(8, 2, 32, 256)

            @pl.when(k == 0)
            def _():
                acc[zs] = p

            @pl.when(k > 0)
            def _():
                acc[zs] += p

            return carry

        lax.fori_loop(0, 4, step, 0)
        j = 2 * (xh * NZ + zs) + xl
        lanes = pl.ds(pl.multiple_of(par * 256, 256), 256)
        dst = out.at[:, j, :, lanes]
        for q, (dx, dp) in enumerate(group):
            u = ((x + dx) % 4) * 2 + ((1 - par) if dp else par)
            start(remote(acc.at[zs, u], dst, c_send.at[q, k_slot], c_recv.at[q, k_slot], group_dev(dx, dp)))
        own = pltpu.make_async_copy(acc.at[zs, own_u], dst, own_sem.at[k_slot])
        own.start()
        locals_.append(own)

    locals_ = []
    own_w.wait()
    relay(0)

    um, up = xm * 2 + par, xp * 2 + par
    uy, umy, upy = x * 2 + 1 - par, xm * 2 + 1 - par, xp * 2 + 1 - par
    u2, u2y = ((x + 2) % 4) * 2 + par, ((x + 2) % 4) * 2 + 1 - par
    t_wait(um, None, 1)
    t_copy(um, 0, 5, dev_xp)
    t_wait(up, None, 3)
    t_copy(up, 1, 7, dev_xm)
    t_wait(uy, None, 0)
    t_copy(uy, None, 2, dev_xp)
    t_copy(uy, None, 4, dev_xm)
    load_t.wait()
    relay(1)
    t_wait(umy, None, 2)
    t_copy(umy, 0, 6, dev_xp)
    t_wait(upy, None, 4)
    t_copy(upy, 1, 8, dev_xm)
    t_wait(u2, 0, 5)
    t_wait(u2, 1, 7)
    t_wait(u2y, 0, 6)
    t_wait(u2y, 1, 8)
    lax.fori_loop(0, 8, lambda u, c: (convert(u), c)[1], 0)
    partner_wait(0, 0)
    compute(0, 0)
    for n in (1, 2, 3):
        if n > 1:
            relay(n)
        for d in range(2):
            partner_wait(d, n)
            compute(d, n)
    for ch in range(4):
        d = 0 if ch < 3 else 1
        ring_wait(d, 4, ch)
        to_partner(d, 4, ch)
    partner_wait(0, 4)
    compute(0, 4)

    for cp in pending:
        cp.wait_send()
    for cp in locals_:
        cp.wait()
    for q in range(7):
        for k in range(8):
            v = out.at[:, k, :, pl.ds(0, 256)]
            remote(v, v, c_send.at[q, k], c_recv.at[q, k], partner).wait_recv()


def body(amplitudes, integrals, occ_energy, vir_energy):
    dma = pltpu.SemaphoreType.DMA
    f32, bf16 = jnp.float32, jnp.bfloat16
    cycle = pl.pallas_call(
        kernel,
        out_shape=jax.ShapeDtypeStruct((2, 32, 32, 512), f32),
        in_specs=[pl.BlockSpec(memory_space=pl.ANY)] * 2,
        out_specs=pl.BlockSpec(memory_space=pl.ANY),
        scratch_shapes=[
            pltpu.VMEM((4, 32, 2, 512), f32),
            pltpu.VMEM((2, 2, 4, 32, 256), f32),
            pltpu.VMEM((8, 4, 8, 2, 32, 256), f32),
            pltpu.VMEM((8, 2, 4, 32, 512), f32),
            pltpu.VMEM((4, 512, 512), bf16),
            pltpu.VMEM((4, 512, 512), bf16),
            pltpu.VMEM((8, 8, 2, 32, 256), f32),
            dma((3,)), dma((8,)), dma((8,)), dma((2, 4, 4)), dma((2, 4, 4)), dma((8, 4)), dma((8, 4)),
            dma((9,)), dma((9,)), dma((7, 8)), dma((7, 8)), dma((8,)),
        ],
        compiler_params=pltpu.CompilerParams(
            collective_id=0, has_side_effects=True, vmem_limit_bytes=60 * 2**20
        ),
    )(amplitudes, integrals)
    rows_i, a_local = cycle.shape[0], cycle.shape[2]
    occ_local = lax.dynamic_slice_in_dim(occ_energy, lax.axis_index("row") * rows_i, rows_i, 0)
    vir_local = lax.dynamic_slice_in_dim(vir_energy, lax.axis_index("col") * a_local, a_local, 0)
    denom = (
        occ_local[:, None, None, None]
        + occ_energy[None, :, None, None]
        - vir_local[None, None, :, None]
        - vir_energy[None, None, None, :]
    )
    return cycle / denom


def solution(mesh):
    return jax.shard_map(
        body,
        mesh=mesh,
        in_specs=(P("row", None, "col", None), P(None, "row", "col", None), P(), P()),
        out_specs=P("row", None, "col", None),
        check_vma=False,
    )
```

time: 365 us -> 125 us (0.34)
  waiting for transfers between devices: 259 us -> 0 us
  Pallas kernels: 0 us -> 118 us
  matrix products: 32.5 us -> 0 us
  blocking collectives: 26.7 us -> 0 us
  local copies, waits for them, and re-layouts: 24.2 us -> 1.5 us
  between operations: 13.5 us -> 0.02 us
  starting transfers between devices: 4.71 us -> 0 us
    all_gather x2 -> x0, waiting for transfers between devices: 163 us -> none  [the longest x1 137 us: body(): panel = lax.all_gather(moved, 'col', axis=3, tiled=True)]
    pallas_call x0 -> x1, Pallas kernels: none -> 118 us  [body(): pl.pallas_call(kernel, out_shape=jax.ShapeDtypeStruct((2, 32, 32, 512), f...]
    all_to_all x1 -> x0, waiting for transfers between devices: 95.9 us -> none  [body(): back = lax.all_to_all(cycle, 'col', split_axis=2, concat_axis=1, tiled=True)]
    dot_general x1 -> x0, matrix products: 32.5 us -> none  [body(): jnp.einsum('ikac,kcjb->ijab', panel, lax.all_gather(integrals, 'row', axi...]
    all_to_all x1 -> x0, blocking collectives: 26.7 us -> none  [body(): lax.all_to_all(amplitudes, 'col', split_axis=3, concat_axis=2, tiled=True)]
    all_to_all x5 -> x0, local copies, waits for them, and re-layouts: 10.4 us -> none  [the longest x3 6.02 us: body(): lax.all_to_all(amplitudes, 'col', split_axis=3, concat_axis=2, tiled=True)]
    transpose x1 -> x0, local copies, waits for them, and re-layouts: 7.32 us -> none  [body(): jnp.einsum('ikac,kcjb->ijab', panel, lax.all_gather(integrals, 'row', axi...]
    unnamed x8 -> x2, local copies, waits for them, and re-layouts: 6.36 us -> 0.01 us
  transfers between devices with their start and end apart: 3 -> 0, of which waited for: 3 -> 0; matrix products, arithmetic and copies ran while one was open for 3% -> 0% of each run, Pallas kernels for 0% -> 0%
where the time goes in v1:
time: 125 us
  Pallas kernels  118 us (94%)
  other arithmetic  5.62 us (4%)
  local copies, waits for them, and re-layouts  1.5 us (1%)
    pallas_call x1, Pallas kernels, body(): pl.pallas_call(kernel, out_shape=jax.ShapeDtypeStruct((2, 32, 32, 512), f...  118 us
    div x1, other arithmetic, body(): return cycle / denom  4.82 us

profile of v1, /device:TPU:1, one launch (start us, length us, event | category | flops | bytes accessed | tf_op | source)
XLA Modules:
  0.0 124.7 jit_solution(14655101805274817217)
XLA Ops:
  0.0 0.0 copy-start
  0.0 0.7 dynamic_slice.6
  0.7 0.8 dynamic_slice.7
  1.5 0.7 broadcast_add_fusion
  2.2 0.1 broadcast_subtract_fusion
  2.3 117.6 %shard_map.46 = f32[2,32,32,512]{3,2,1,0:T(8,128)} custom-call(f32[2,4,32,512]{3,2,1,0:T(8,128)} %t_hbm.1, f32[4,32,2,512]{3,2,1,0:T(2,128)} %w_hbm.1), custom_call_target="tpu_custom_call" | custom-call | tf_op jit(solution)/shard_map/pallas_call | solution.py:251
  119.9 0.0 copy-done
  119.9 4.8 %subtract_divide_fusion = f32[2,32,32,512]{3,2,1,0:T(8,128)} fusion(f32[2,32,32,512]{3,2,1,0:T(8,128)} %shard_map.46, f32[512]{0:T(512)S(1)} %copy-done, f32[2,32,32]{2,1,0:T(8,128)S(1)} %broadcast_subtract_fusion), kind=kLoop, calls=%fused_computation | loop fusion | flops 2097152 | bytes 8398848 | tf_op jit(solution)/shard_map/div | solution.py:280
Async XLA Ops:
  0.0 119.9 %copy-start = (f32[512]{0:T(512)S(1)}, f32[512]{0:T(512)}, u32[]{:S(2)}) copy-start(f32[512]{0:T(512)} %param.7) | copy-start | bytes 6148

commit v2 on v0

v2 whole, which is shorter than its diff:
```python
import jax
import jax.numpy as jnp
from jax import lax
from jax.experimental import pallas as pl
from jax.experimental.pallas import tpu as pltpu
from jax.sharding import PartitionSpec as P

MESH = pl.DeviceIdType.MESH
NZ = 8
NEAR = ((0, 0), (1, 1), (1, 3), (1, 0), (0, 2), (0, 1), (0, 3), (3, 0))


def place(x, y, z, core):
    return (y * 4 + (x % 2) * 2 + core, (x // 2) * NZ + z)


def flip(v, bits):
    for b in range(3):
        if (bits >> b) & 1:
            v = v + (1 << b) * (1 - 2 * ((v // (1 << b)) % 2))
    return v


def kernel(t_hbm, w_hbm, occ, vir, out, w_raw, w_src, w_buf, t_buf, t_hi, t_lo, acc, vir_a,
           load_sem, pre_send, pre_recv, ring_send, ring_recv, part_send, part_recv,
           t_send, t_recv, c_send, c_recv, own_sem):
    row, col = lax.axis_index("row"), lax.axis_index("col")
    y, xl, core = row // 4, (row // 2) % 2, row % 2
    xh, z = col // NZ, col % NZ
    x = xh * 2 + xl
    s = y * 2 + xl
    far = y // 2
    from_xh = xh + far * (1 - 2 * xh)
    half = y % 2
    z_next = ((z + 1) % NZ, (z + NZ - 1) % NZ)
    partner = place(x, y, z, 1 - core)
    pending, locals_ = [], []

    def remote(src, dst, send, recv, device):
        return pltpu.make_async_remote_copy(src, dst, send, recv, device_id=device, device_id_type=MESH)

    def start(cp):
        cp.start()
        pending.append(cp)

    def arrived(view, recv):
        remote(view, view, load_sem.at[0], recv, partner).wait_recv()

    load_w = pltpu.make_async_copy(w_hbm, w_raw, load_sem.at[0])
    load_w.start()
    load_t = pltpu.make_async_copy(t_hbm, t_buf.at[0], load_sem.at[1])
    load_t.start()

    barrier = pltpu.get_barrier_semaphore()
    everyone = [place((x + dx) % 4, (y + dy) % 4, z, core)
                for dx in range(4) for dy in range(4) if (dx, dy) != (0, 0)]
    everyone += [place(x, y, z_next[0], core), place(x, y, z_next[1], core), partner]
    for d in everyone:
        pl.semaphore_signal(barrier, inc=1, device_id=d, device_id_type=MESH)

    load_w.wait()
    for k in range(4):
        for jj in range(2):
            for bh in range(2):
                w_src[jj, bh, k] = w_raw[k, :, jj, bh * 256:bh * 256 + 256]
    pl.semaphore_wait(barrier, len(everyone))

    def pre(e):
        se = flip(s, e)
        ye, xe = se // 2, se % 2
        xhe = xh + (ye // 2) * (1 - 2 * xh)
        return remote(w_src.at[xe, ye % 2], w_buf.at[z, :, s, core], pre_send.at[e], pre_recv.at[e],
                      place(xhe * 2 + xe, ye, z, core))

    def pre_wait(e, se):
        arrived(w_buf.at[z, :, se, core], pre_recv.at[e])

    own_w = pltpu.make_async_copy(w_src.at[xl, half], w_buf.at[z, :, s, core], pre_recv.at[0])
    first = pre(0)

    @pl.when(far == 0)
    def _():
        own_w.start()

    start(pre(1))

    @pl.when(far == 1)
    def _():
        first.start()

    for e in (2, 3, 6, 7, 4, 5):
        start(pre(e))

    for r, (dx, dy) in enumerate(NEAR):
        if r > 0:
            start(remote(t_hbm, t_buf.at[r], t_send.at[r], t_recv.at[r],
                         place((x + dx) % 4, (y + dy) % 4, z, core)))

    s0 = flip(s, 1) * far + s * (1 - far)
    chunks = [(s0, 1), (flip(s0, 1), 1)] + [((flip(s, e) // 2) * 2, 2) for e in (2, 6, 4)]

    def w_view(zs, ch, which):
        base, size = chunks[ch]
        return w_buf.at[zs, :, pl.ds(base, size), which]

    def slice_at(d, n):
        return (z + NZ - n) % NZ if d == 0 else (z + n) % NZ

    def slot_of(d, n):
        return 0 if n == 0 else 7 if n == 4 else 2 * n - 1 + d

    def goes_on(d, n, ch):
        return n < 3 or (n == 3 and ((ch < 3) if d == 0 else (ch >= 3)))

    def relay(n, ch):
        if n == 0:
            if ch == 0:
                pre_wait(far, s0)
            elif ch == 1:
                pre_wait(1 - far, flip(s0, 1))
            else:
                e = (2, 6, 4)[ch - 2]
                pre_wait(e, flip(s, e))
                pre_wait(e + 1, flip(s, e + 1))
        for d in range(2):
            if n == 4 and d != (0 if ch < 3 else 1):
                continue
            v = w_view(slice_at(d, n), ch, core)
            if n > 0:
                arrived(v, ring_recv.at[d, n - 1, ch])
            if goes_on(d, n, ch):
                start(remote(v, v, ring_send.at[d, n, ch], ring_recv.at[d, n, ch],
                             place(x, y, z_next[d], core)))
            if n > 0 or d == 0:
                k = slot_of(d, n)
                start(remote(v, v, part_send.at[k, ch], part_recv.at[k, ch], partner))

    def partner_wait(d, n):
        for ch in range(5):
            arrived(w_view(slice_at(d, n), ch, 1 - core), part_recv.at[slot_of(d, n), ch])

    def convert(r):
        for i in range(2):
            for k in range(4):
                v = t_buf[r, i, k]
                hi = v.astype(jnp.bfloat16)
                rows = pl.ds(r * 64 + i * 32, 32)
                t_hi[k, rows, :] = hi
                t_lo[k, rows, :] = (v - hi.astype(jnp.float32)).astype(jnp.bfloat16)

    lane = lax.broadcasted_iota(jnp.int32, (32, 512), 1)
    sub = lax.broadcasted_iota(jnp.int32, (32, 512), 0)
    vir_row = jnp.broadcast_to(vir[...], (32, 512))
    for h in range(2):
        picked = jnp.where(lane == sub + (h * NZ + z) * 32, vir_row, 0.0)
        vir_a[h] = jnp.broadcast_to(jnp.sum(picked, axis=1, keepdims=True), (32, 128))

    def compute(d, n):
        zs = slice_at(d, n)
        k_slot = slot_of(d, n)
        partner_wait(d, n)

        def step(k, carry):
            w = w_buf[zs, k].reshape(512, 256)
            w_hi = w.astype(jnp.bfloat16)
            w_lo = (w - w_hi.astype(jnp.float32)).astype(jnp.bfloat16)
            p = jnp.dot(t_hi[k], w_hi, preferred_element_type=jnp.float32)
            p += jnp.dot(t_lo[k], w_hi, preferred_element_type=jnp.float32)
            p += jnp.dot(t_hi[k], w_lo, preferred_element_type=jnp.float32)
            p = p.reshape(8, 2, 32, 256)

            @pl.when(k == 0)
            def _():
                acc[zs] = p

            @pl.when(k > 0)
            def _():
                acc[zs] += p

            return carry

        lax.fori_loop(0, 4, step, 0)
        j = 2 * (from_xh * NZ + zs) + xl
        lanes = pl.ds(pl.multiple_of(half * 256, 256), 256)
        dst = out.at[:, j, :, lanes]
        vir_b = vir[:, lanes]
        occ_j = occ[j]
        order = list(range(1, 8)) + [0]
        for r in order:
            dx, dy = NEAR[r]
            xo, yo = (x + 4 - dx) % 4, (y + 4 - dy) % 4
            column = vir_a[xo // 2]
            column = jnp.concatenate([column, column], axis=1)
            for i in range(2):
                occ_i = occ[(yo * 4 + (xo % 2) * 2 + core) * 2 + i]
                denom = ((occ_i + occ_j) - column) - vir_b
                acc[zs, r, i] = acc[zs, r, i] / denom
        for r in order:
            dx, dy = NEAR[r]
            if r > 0:
                start(remote(acc.at[zs, r], dst, c_send.at[r, k_slot], c_recv.at[r, k_slot],
                             place((x + 4 - dx) % 4, (y + 4 - dy) % 4, z, core)))
            else:
                own = pltpu.make_async_copy(acc.at[zs, r], dst, own_sem.at[k_slot])
                own.start()
                locals_.append(own)

    def relays(n, *chs):
        for ch in chs:
            relay(n, ch)

    def t_ready(*rs):
        for r in rs:
            arrived(t_buf.at[r], t_recv.at[r])
            convert(r)

    relays(0, 0, 1, 2, 3, 4)
    load_t.wait()
    convert(0)
    relays(1, 0, 1, 2, 3, 4)
    t_ready(1, 2, 3)
    relays(2, 0, 1, 2)
    t_ready(4, 5, 6, 7)
    relays(2, 3)
    compute(0, 0)
    relays(2, 4)
    compute(0, 1)
    compute(1, 1)
    relays(3, 0)
    compute(0, 2)
    relays(3, 1)
    compute(1, 2)
    relays(3, 2, 3, 4)
    compute(0, 3)
    compute(1, 3)
    relays(4, 0, 1, 3, 2, 4)
    compute(0, 4)

    for cp in pending:
        cp.wait_send()

    @pl.when(far == 1)
    def _():
        first.wait_send()

    for cp in locals_:
        cp.wait()
    for r in range(1, 8):
        for k in range(8):
            arrived(out.at[:, k, :, pl.ds(0, 256)], c_recv.at[r, k])


def body(amplitudes, integrals, occ_energy, vir_energy):
    dma = pltpu.SemaphoreType.DMA
    f32, bf16 = jnp.float32, jnp.bfloat16
    hbm = pl.BlockSpec(memory_space=pl.ANY)
    return pl.pallas_call(
        kernel,
        out_shape=jax.ShapeDtypeStruct((2, 32, 32, 512), f32),
        in_specs=[hbm, hbm, pl.BlockSpec(memory_space=pltpu.SMEM), pl.BlockSpec(memory_space=pltpu.VMEM)],
        out_specs=OUT_SPEC,
        scratch_shapes=[
            pltpu.VMEM((4, 32, 2, 512), f32),
            pltpu.VMEM((2, 2, 4, 32, 256), f32),
            pltpu.VMEM((8, 4, 8, 2, 32, 256), f32),
            pltpu.VMEM((8, 2, 4, 32, 512), f32),
            pltpu.VMEM((4, 512, 512), bf16),
            pltpu.VMEM((4, 512, 512), bf16),
            pltpu.VMEM((8, 8, 2, 32, 256), f32),
            pltpu.VMEM((2, 32, 128), f32),
            dma((2,)), dma((8,)), dma((8,)), dma((2, 4, 5)), dma((2, 4, 5)), dma((8, 5)), dma((8, 5)),
            dma((8,)), dma((8,)), dma((8, 8)), dma((8, 8)), dma((8,)),
        ],
        compiler_params=pltpu.CompilerParams(
            collective_id=0, has_side_effects=True, vmem_limit_bytes=60 * 2**20
        ),
    )(amplitudes, integrals, occ_energy, vir_energy.reshape(1, -1))


OUT_SPEC = pl.BlockSpec(memory_space=pl.ANY)


def solution(mesh):
    return jax.shard_map(
        body,
        mesh=mesh,
        in_specs=(P("row", None, "col", None), P(None, "row", "col", None), P(), P()),
        out_specs=P("row", None, "col", None),
        check_vma=False,
    )
```

time: 365 us -> 126 us (0.35)
  waiting for transfers between devices: 259 us -> 0 us
  Pallas kernels: 0 us -> 121 us
  matrix products: 32.5 us -> 0 us
  blocking collectives: 26.7 us -> 0 us
  local copies, waits for them, and re-layouts: 24.2 us -> 5.01 us
  between operations: 13.5 us -> 0.01 us
  starting transfers between devices: 4.71 us -> 0 us
  other arithmetic: 4.68 us -> 0 us
    all_gather x2 -> x0, waiting for transfers between devices: 163 us -> none  [the longest x1 137 us: body(): panel = lax.all_gather(moved, 'col', axis=3, tiled=True)]
    pallas_call x0 -> x1, Pallas kernels: none -> 121 us  [body(): pl.pallas_call(kernel, out_shape=jax.ShapeDtypeStruct((2, 32, 32, 512), f...]
    all_to_all x1 -> x0, waiting for transfers between devices: 95.9 us -> none  [body(): back = lax.all_to_all(cycle, 'col', split_axis=2, concat_axis=1, tiled=True)]
    dot_general x1 -> x0, matrix products: 32.5 us -> none  [body(): jnp.einsum('ikac,kcjb->ijab', panel, lax.all_gather(integrals, 'row', axi...]
    all_to_all x1 -> x0, blocking collectives: 26.7 us -> none  [body(): lax.all_to_all(amplitudes, 'col', split_axis=3, concat_axis=2, tiled=True)]
    all_to_all x5 -> x0, local copies, waits for them, and re-layouts: 10.4 us -> none  [the longest x3 6.02 us: body(): lax.all_to_all(amplitudes, 'col', split_axis=3, concat_axis=2, tiled=True)]
    transpose x1 -> x0, local copies, waits for them, and re-layouts: 7.32 us -> none  [body(): jnp.einsum('ikac,kcjb->ijab', panel, lax.all_gather(integrals, 'row', axi...]
    all_to_all x1 -> x0, starting transfers between devices: 4.67 us -> none  [body(): back = lax.all_to_all(cycle, 'col', split_axis=2, concat_axis=1, tiled=True)]
  transfers between devices with their start and end apart: 3 -> 0, of which waited for: 3 -> 0; matrix products, arithmetic and copies ran while one was open for 3% -> 0% of each run, Pallas kernels for 0% -> 0%
where the time goes in v2:
time: 126 us
  Pallas kernels  121 us (96%)
  local copies, waits for them, and re-layouts  5.01 us (4%)
    pallas_call x1, Pallas kernels, body(): pl.pallas_call(kernel, out_shape=jax.ShapeDtypeStruct((2, 32, 32, 512), f...  121 us
    unnamed x1, local copies, waits for them, and re-layouts  5.01 us

profile of v2, /device:TPU:1, one launch (start us, length us, event | category | flops | bytes accessed | tf_op | source)
XLA Modules:
  0.0 126.1 jit_solution(477390997461687178)
XLA Ops:
  0.0 121.1 %shard_map.46 = f32[2,32,32,512]{3,2,1,0:T(8,128)} custom-call(f32[2,4,32,512]{3,2,1,0:T(8,128)} %t_hbm.1, f32[4,32,2,512]{3,2,1,0:T(2,128)} %w_hbm.1, f32[32]{0:T(128)} %occ.1, f32[1,512]{1,0:T(1,128)} %bitcast.1), custom_call_target="tpu_custom_call" | custom-call | tf_op jit(solution)/shard_map/pallas_call | solution.py:257
  121.1 5.0 %copy.6 = f32[2,32,32,512]{3,2,1,0:T(8,128)} copy(f32[2,32,32,512]{3,2,1,0:T(8,128)} %shard_map.46) | data formatting | bytes 8388608

commit v3 on v2

--- a/solution.py
+++ b/solution.py
@@ -7,7 +7,6 @@
 
 MESH = pl.DeviceIdType.MESH
 NZ = 8
-NEAR = ((0, 0), (1, 1), (1, 3), (1, 0), (0, 2), (0, 1), (0, 3), (3, 0))
 
 
 def place(x, y, z, core):
@@ -29,9 +28,11 @@
     xh, z = col // NZ, col % NZ
     x = xh * 2 + xl
     s = y * 2 + xl
-    far = y // 2
-    from_xh = xh + far * (1 - 2 * xh)
-    half = y % 2
+    block = (y + 2 * xl) % 4
+    jj, bh = block // 2, block % 2
+    inner, outer = 1 + 2 * xl, 3 - 2 * xl
+    THERE = ((0, 0), (outer, 0), (outer, 1), (outer, 3), (2, 0), (inner, 0), (0, 1), (0, 3))
+    BACK = ((0, 0), (outer, 0), (outer, 3), (outer, 1), (2, 0), (inner, 0), (0, 3), (0, 1))
     z_next = ((z + 1) % NZ, (z + NZ - 1) % NZ)
     partner = place(x, y, z, 1 - core)
     pending, locals_ = [], []
@@ -60,44 +61,33 @@
 
     load_w.wait()
     for k in range(4):
-        for jj in range(2):
-            for bh in range(2):
-                w_src[jj, bh, k] = w_raw[k, :, jj, bh * 256:bh * 256 + 256]
+        for b in range(4):
+            w_src[b // 2, b % 2, k] = w_raw[k, :, b // 2, (b % 2) * 256:(b % 2) * 256 + 256]
     pl.semaphore_wait(barrier, len(everyone))
 
     def pre(e):
         se = flip(s, e)
         ye, xe = se // 2, se % 2
-        xhe = xh + (ye // 2) * (1 - 2 * xh)
-        return remote(w_src.at[xe, ye % 2], w_buf.at[z, :, s, core], pre_send.at[e], pre_recv.at[e],
-                      place(xhe * 2 + xe, ye, z, core))
-
-    def pre_wait(e, se):
-        arrived(w_buf.at[z, :, se, core], pre_recv.at[e])
-
-    own_w = pltpu.make_async_copy(w_src.at[xl, half], w_buf.at[z, :, s, core], pre_recv.at[0])
-    first = pre(0)
-
-    @pl.when(far == 0)
-    def _():
-        own_w.start()
-
-    start(pre(1))
-
-    @pl.when(far == 1)
-    def _():
-        first.start()
-
-    for e in (2, 3, 6, 7, 4, 5):
-        start(pre(e))
-
-    for r, (dx, dy) in enumerate(NEAR):
-        if r > 0:
+        be = (ye + 2 * xe) % 4
+        return remote(w_src.at[be // 2, be % 2], w_buf.at[z, :, s, core], pre_send.at[e], pre_recv.at[e],
+                      place(xh * 2 + xe, ye, z, core))
+
+    def pre_wait(e):
+        arrived(w_buf.at[z, :, flip(s, e), core], pre_recv.at[e])
+
+    own_w = pltpu.make_async_copy(w_src.at[jj, bh], w_buf.at[z, :, s, core], load_sem.at[2])
+    own_w.start()
+
+    def send_t(*rs):
+        for r in rs:
+            dx, dy = THERE[r]
             start(remote(t_hbm, t_buf.at[r], t_send.at[r], t_recv.at[r],
                          place((x + dx) % 4, (y + dy) % 4, z, core)))
 
-    s0 = flip(s, 1) * far + s * (1 - far)
-    chunks = [(s0, 1), (flip(s0, 1), 1)] + [((flip(s, e) // 2) * 2, 2) for e in (2, 6, 4)]
+    def t_relay(r, dy):
+        start(remote(t_buf.at[1], t_buf.at[r], t_send.at[r], t_recv.at[r], place(x, (y + dy) % 4, z, core)))
+
+    chunks = [(s, 1), (flip(s, 1), 1)] + [((flip(s, e) // 2) * 2, 2) for e in (2, 6, 4)]
 
     def w_view(zs, ch, which):
         base, size = chunks[ch]
@@ -114,26 +104,23 @@
 
     def relay(n, ch):
         if n == 0:
-            if ch == 0:
-                pre_wait(far, s0)
-            elif ch == 1:
-                pre_wait(1 - far, flip(s0, 1))
-            else:
-                e = (2, 6, 4)[ch - 2]
-                pre_wait(e, flip(s, e))
-                pre_wait(e + 1, flip(s, e + 1))
+            for e in ((), (1,), (2, 3), (6, 7), (4, 5))[ch]:
+                pre_wait(e)
         for d in range(2):
             if n == 4 and d != (0 if ch < 3 else 1):
                 continue
             v = w_view(slice_at(d, n), ch, core)
             if n > 0:
                 arrived(v, ring_recv.at[d, n - 1, ch])
+            source = v
+            if n == 0 and ch == 0:
+                source, v = w_src.at[jj, bh], w_buf.at[z, :, s, core]
             if goes_on(d, n, ch):
-                start(remote(v, v, ring_send.at[d, n, ch], ring_recv.at[d, n, ch],
+                start(remote(source, v, ring_send.at[d, n, ch], ring_recv.at[d, n, ch],
                              place(x, y, z_next[d], core)))
             if n > 0 or d == 0:
                 k = slot_of(d, n)
-                start(remote(v, v, part_send.at[k, ch], part_recv.at[k, ch], partner))
+                start(remote(source, v, part_send.at[k, ch], part_recv.at[k, ch], partner))
 
     def partner_wait(d, n):
         for ch in range(5):
@@ -180,15 +167,15 @@
             return carry
 
         lax.fori_loop(0, 4, step, 0)
-        j = 2 * (from_xh * NZ + zs) + xl
-        lanes = pl.ds(pl.multiple_of(half * 256, 256), 256)
+        j = 2 * (xh * NZ + zs) + jj
+        lanes = pl.ds(pl.multiple_of(bh * 256, 256), 256)
         dst = out.at[:, j, :, lanes]
         vir_b = vir[:, lanes]
         occ_j = occ[j]
-        order = list(range(1, 8)) + [0]
+        order = (2, 3, 4, 1, 5, 6, 7, 0)
         for r in order:
-            dx, dy = NEAR[r]
-            xo, yo = (x + 4 - dx) % 4, (y + 4 - dy) % 4
+            dx, dy = BACK[r]
+            xo, yo = (x + dx) % 4, (y + dy) % 4
             column = vir_a[xo // 2]
             column = jnp.concatenate([column, column], axis=1)
             for i in range(2):
@@ -196,10 +183,10 @@
                 denom = ((occ_i + occ_j) - column) - vir_b
                 acc[zs, r, i] = acc[zs, r, i] / denom
         for r in order:
-            dx, dy = NEAR[r]
+            dx, dy = BACK[r]
             if r > 0:
                 start(remote(acc.at[zs, r], dst, c_send.at[r, k_slot], c_recv.at[r, k_slot],
-                             place((x + 4 - dx) % 4, (y + 4 - dy) % 4, z, core)))
+                             place((x + dx) % 4, (y + dy) % 4, z, core)))
             else:
                 own = pltpu.make_async_copy(acc.at[zs, r], dst, own_sem.at[k_slot])
                 own.start()
@@ -214,14 +201,24 @@
             arrived(t_buf.at[r], t_recv.at[r])
             convert(r)
 
-    relays(0, 0, 1, 2, 3, 4)
+    relays(0, 0)
+    for e in (1, 2, 3, 6, 7, 4, 5):
+        start(pre(e))
+    send_t(1)
+    relays(0, 1, 2, 3, 4)
+    send_t(6, 7, 5, 4)
     load_t.wait()
     convert(0)
-    relays(1, 0, 1, 2, 3, 4)
-    t_ready(1, 2, 3)
+    relays(1, 0)
+    t_ready(1)
+    t_relay(2, 1)
+    t_relay(3, 3)
+    relays(1, 1, 2, 3, 4)
+    t_ready(5, 6, 7)
     relays(2, 0, 1, 2)
-    t_ready(4, 5, 6, 7)
+    t_ready(4, 2, 3)
     relays(2, 3)
+    own_w.wait()
     compute(0, 0)
     relays(2, 4)
     compute(0, 1)
@@ -238,11 +235,6 @@
 
     for cp in pending:
         cp.wait_send()
-
-    @pl.when(far == 1)
-    def _():
-        first.wait_send()
-
     for cp in locals_:
         cp.wait()
     for r in range(1, 8):
@@ -253,12 +245,12 @@
 def body(amplitudes, integrals, occ_energy, vir_energy):
     dma = pltpu.SemaphoreType.DMA
     f32, bf16 = jnp.float32, jnp.bfloat16
-    hbm = pl.BlockSpec(memory_space=pl.ANY)
+    hbm = pl.BlockSpec(memory_space=pltpu.HBM)
     return pl.pallas_call(
         kernel,
         out_shape=jax.ShapeDtypeStruct((2, 32, 32, 512), f32),
         in_specs=[hbm, hbm, pl.BlockSpec(memory_space=pltpu.SMEM), pl.BlockSpec(memory_space=pltpu.VMEM)],
-        out_specs=OUT_SPEC,
+        out_specs=pl.BlockSpec(memory_space=pl.ANY),
         scratch_shapes=[
             pltpu.VMEM((4, 32, 2, 512), f32),
             pltpu.VMEM((2, 2, 4, 32, 256), f32),
@@ -268,16 +260,14 @@
             pltpu.VMEM((4, 512, 512), bf16),
             pltpu.VMEM((8, 8, 2, 32, 256), f32),
             pltpu.VMEM((2, 32, 128), f32),
-            dma((2,)), dma((8,)), dma((8,)), dma((2, 4, 5)), dma((2, 4, 5)), dma((8, 5)), dma((8, 5)),
+            dma((3,)), dma((8,)), dma((8,)), dma((2, 4, 5)), dma((2, 4, 5)), dma((8, 5)), dma((8, 5)),
             dma((8,)), dma((8,)), dma((8, 8)), dma((8, 8)), dma((8,)),
         ],
         compiler_params=pltpu.CompilerParams(
-            collective_id=0, has_side_effects=True, vmem_limit_bytes=60 * 2**20
+            collective_id=0, has_side_effects=True, vmem_limit_bytes=48 * 2**20
         ),
-    )(amplitudes, integrals, occ_energy, vir_energy.reshape(1, -1))
-
-
-OUT_SPEC = pl.BlockSpec(memory_space=pl.ANY)
+    )(*(pltpu.with_memory_space_constraint(v, pltpu.HBM)
+        for v in (amplitudes, integrals, occ_energy, vir_energy.reshape(1, -1))))
 
 
 def solution(mesh):

time: 126 us -> 112 us (0.89)
  Pallas kernels: 121 us -> 110 us
  local copies, waits for them, and re-layouts: 5.01 us -> 2.02 us
    pallas_call x1, Pallas kernels: 121 us -> 110 us  [body(): pl.pallas_call(kernel, out_shape=jax.ShapeDtypeStruct((2, 32, 32, 512), f...]
    unnamed x1, local copies, waits for them, and re-layouts: 5.01 us -> 2.02 us
where the time goes in v3:
time: 112 us
  Pallas kernels  110 us (98%)
  local copies, waits for them, and re-layouts  2.02 us (2%)
    pallas_call x1, Pallas kernels, body(): pl.pallas_call(kernel, out_shape=jax.ShapeDtypeStruct((2, 32, 32, 512), f...  110 us

profile of v3, /device:TPU:1, one launch (start us, length us, event | category | flops | bytes accessed | tf_op | source)
XLA Modules:
  0.0 111.8 jit_solution(8527740816843134741)
XLA Ops:
  0.0 109.7 %shard_map.46 = f32[2,32,32,512]{3,2,1,0:T(8,128)S(1)} custom-call(f32[2,4,32,512]{3,2,1,0:T(8,128)} %t_hbm.1, f32[4,32,2,512]{3,2,1,0:T(2,128)} %w_hbm.1, f32[32]{0:T(128)} %occ.1, f32[1,512]{1,0:T(1,128)} %bitcast.1), custom_call_target="tpu_custom_call" | custom-call | tf_op jit(solution)/shard_map/pallas_call | solution.py:249
  109.7 2.0 %copy.6 = f32[2,32,32,512]{3,2,1,0:T(8,128)} copy(f32[2,32,32,512]{3,2,1,0:T(8,128)S(1)} %shard_map.46) | data formatting | bytes 8388608

commit v4 on v3

--- a/solution.py
+++ b/solution.py
@@ -7,6 +7,7 @@
 
 MESH = pl.DeviceIdType.MESH
 NZ = 8
+SHARED_FROM = 2
 
 
 def place(x, y, z, core):
@@ -22,7 +23,7 @@
 
 def kernel(t_hbm, w_hbm, occ, vir, out, w_raw, w_src, w_buf, t_buf, t_hi, t_lo, acc, vir_a,
            load_sem, pre_send, pre_recv, ring_send, ring_recv, part_send, part_recv,
-           t_send, t_recv, c_send, c_recv, own_sem):
+           swap_send, swap_recv, t_send, t_recv, c_send, c_recv, own_sem):
     row, col = lax.axis_index("row"), lax.axis_index("col")
     y, xl, core = row // 4, (row // 2) % 2, row % 2
     xh, z = col // NZ, col % NZ
@@ -35,6 +36,7 @@
     BACK = ((0, 0), (outer, 0), (outer, 3), (outer, 1), (2, 0), (inner, 0), (0, 3), (0, 1))
     z_next = ((z + 1) % NZ, (z + NZ - 1) % NZ)
     partner = place(x, y, z, 1 - core)
+    twin = place(xh * 2 + 1 - xl, (y + 2) % 4, z, core)
     pending, locals_ = [], []
 
     def remote(src, dst, send, recv, device):
@@ -89,8 +91,10 @@
 
     chunks = [(s, 1), (flip(s, 1), 1)] + [((flip(s, e) // 2) * 2, 2) for e in (2, 6, 4)]
 
-    def w_view(zs, ch, which):
-        base, size = chunks[ch]
+    def w_view(zs, ch, which, n):
+        base, size = chunks[ch] if ch < 5 else (flip(s, 5), 1)
+        if ch == 4 and n >= SHARED_FROM:
+            base, size = flip(s, 4), 1
         return w_buf.at[zs, :, pl.ds(base, size), which]
 
     def slice_at(d, n):
@@ -109,29 +113,44 @@
         for d in range(2):
             if n == 4 and d != (0 if ch < 3 else 1):
                 continue
-            v = w_view(slice_at(d, n), ch, core)
+            v = w_view(slice_at(d, n), ch, core, n)
             if n > 0:
                 arrived(v, ring_recv.at[d, n - 1, ch])
             source = v
             if n == 0 and ch == 0:
                 source, v = w_src.at[jj, bh], w_buf.at[z, :, s, core]
+            k = slot_of(d, n)
             if goes_on(d, n, ch):
-                start(remote(source, v, ring_send.at[d, n, ch], ring_recv.at[d, n, ch],
+                on, to = (source, v)
+                if n > 0 or ch == 4:
+                    on = to = w_view(slice_at(d, n), ch, core, n + 1)
+                start(remote(on, to, ring_send.at[d, n, ch], ring_recv.at[d, n, ch],
                              place(x, y, z_next[d], core)))
+            if n >= SHARED_FROM and ch == 0:
+                start(remote(v, v, swap_send.at[k], swap_recv.at[k], twin))
             if n > 0 or d == 0:
-                k = slot_of(d, n)
                 start(remote(source, v, part_send.at[k, ch], part_recv.at[k, ch], partner))
 
+    def swapped(n):
+        for d in range(2 if n < 4 else 1):
+            k = slot_of(d, n)
+            v = w_view(slice_at(d, n), 5, core, n)
+            arrived(v, swap_recv.at[k])
+            start(remote(v, v, part_send.at[k, 5], part_recv.at[k, 5], partner))
+
     def partner_wait(d, n):
-        for ch in range(5):
-            arrived(w_view(slice_at(d, n), ch, 1 - core), part_recv.at[slot_of(d, n), ch])
+        for ch in range(6 if n >= SHARED_FROM else 5):
+            arrived(w_view(slice_at(d, n), ch, 1 - core, n), part_recv.at[slot_of(d, n), ch])
+
+    def pos(r):
+        return (r + 7) % 8
 
     def convert(r):
         for i in range(2):
             for k in range(4):
                 v = t_buf[r, i, k]
                 hi = v.astype(jnp.bfloat16)
-                rows = pl.ds(r * 64 + i * 32, 32)
+                rows = pl.ds(pos(r) * 64 + i * 32, 32)
                 t_hi[k, rows, :] = hi
                 t_lo[k, rows, :] = (v - hi.astype(jnp.float32)).astype(jnp.bfloat16)
 
@@ -142,55 +161,60 @@
         picked = jnp.where(lane == sub + (h * NZ + z) * 32, vir_row, 0.0)
         vir_a[h] = jnp.broadcast_to(jnp.sum(picked, axis=1, keepdims=True), (32, 128))
 
-    def compute(d, n):
+    def compute(d, n, groups):
         zs = slice_at(d, n)
         k_slot = slot_of(d, n)
-        partner_wait(d, n)
-
-        def step(k, carry):
-            w = w_buf[zs, k].reshape(512, 256)
-            w_hi = w.astype(jnp.bfloat16)
-            w_lo = (w - w_hi.astype(jnp.float32)).astype(jnp.bfloat16)
-            p = jnp.dot(t_hi[k], w_hi, preferred_element_type=jnp.float32)
-            p += jnp.dot(t_lo[k], w_hi, preferred_element_type=jnp.float32)
-            p += jnp.dot(t_hi[k], w_lo, preferred_element_type=jnp.float32)
-            p = p.reshape(8, 2, 32, 256)
-
-            @pl.when(k == 0)
-            def _():
-                acc[zs] = p
-
-            @pl.when(k > 0)
-            def _():
-                acc[zs] += p
-
-            return carry
-
-        lax.fori_loop(0, 4, step, 0)
+        if 0 in groups:
+            partner_wait(d, n)
+
         j = 2 * (xh * NZ + zs) + jj
         lanes = pl.ds(pl.multiple_of(bh * 256, 256), 256)
         dst = out.at[:, j, :, lanes]
         vir_b = vir[:, lanes]
         occ_j = occ[j]
-        order = (2, 3, 4, 1, 5, 6, 7, 0)
-        for r in order:
-            dx, dy = BACK[r]
-            xo, yo = (x + dx) % 4, (y + dy) % 4
-            column = vir_a[xo // 2]
-            column = jnp.concatenate([column, column], axis=1)
-            for i in range(2):
-                occ_i = occ[(yo * 4 + (xo % 2) * 2 + core) * 2 + i]
-                denom = ((occ_i + occ_j) - column) - vir_b
-                acc[zs, r, i] = acc[zs, r, i] / denom
-        for r in order:
-            dx, dy = BACK[r]
-            if r > 0:
-                start(remote(acc.at[zs, r], dst, c_send.at[r, k_slot], c_recv.at[r, k_slot],
-                             place((x + dx) % 4, (y + dy) % 4, z, core)))
-            else:
-                own = pltpu.make_async_copy(acc.at[zs, r], dst, own_sem.at[k_slot])
-                own.start()
-                locals_.append(own)
+        for rs in [((1, 2, 3, 4), (5, 6, 7, 0))[g] for g in groups]:
+            p0, np_ = pos(rs[0]), len(rs)
+
+            def step(k, carry):
+                w = w_buf[zs, k].reshape(512, 256)
+                w_hi = w.astype(jnp.bfloat16)
+                w_lo = (w - w_hi.astype(jnp.float32)).astype(jnp.bfloat16)
+                hi, lo = t_hi[k, p0 * 64:(p0 + np_) * 64, :], t_lo[k, p0 * 64:(p0 + np_) * 64, :]
+                p = jnp.dot(hi, w_hi, preferred_element_type=jnp.float32)
+                p += jnp.dot(lo, w_hi, preferred_element_type=jnp.float32)
+                p += jnp.dot(hi, w_lo, preferred_element_type=jnp.float32)
+                p = p.reshape(np_, 2, 32, 256)
+
+                @pl.when(k == 0)
+                def _():
+                    acc[zs, p0:p0 + np_] = p
+
+                @pl.when(k > 0)
+                def _():
+                    acc[zs, p0:p0 + np_] += p
+
+                return carry
+
+            lax.fori_loop(0, 4, step, 0)
+            order = [r for r in (2, 3, 4, 1, 5, 6, 7, 0) if r in rs]
+            for r in order:
+                dx, dy = BACK[r]
+                xo, yo = (x + dx) % 4, (y + dy) % 4
+                column = vir_a[xo // 2]
+                column = jnp.concatenate([column, column], axis=1)
+                for i in range(2):
+                    occ_i = occ[(yo * 4 + (xo % 2) * 2 + core) * 2 + i]
+                    denom = ((occ_i + occ_j) - column) - vir_b
+                    acc[zs, pos(r), i] = acc[zs, pos(r), i] / denom
+            for r in order:
+                dx, dy = BACK[r]
+                if r > 0:
+                    start(remote(acc.at[zs, pos(r)], dst, c_send.at[r, k_slot], c_recv.at[r, k_slot],
+                                 place((x + dx) % 4, (y + dy) % 4, z, core)))
+                else:
+                    own = pltpu.make_async_copy(acc.at[zs, pos(r)], dst, own_sem.at[k_slot])
+                    own.start()
+                    locals_.append(own)
 
     def relays(n, *chs):
         for ch in chs:
@@ -204,34 +228,47 @@
     relays(0, 0)
     for e in (1, 2, 3, 6, 7, 4, 5):
         start(pre(e))
-    send_t(1)
+    send_t(1, 4)
     relays(0, 1, 2, 3, 4)
-    send_t(6, 7, 5, 4)
-    load_t.wait()
-    convert(0)
-    relays(1, 0)
     t_ready(1)
     t_relay(2, 1)
     t_relay(3, 3)
-    relays(1, 1, 2, 3, 4)
+    send_t(6, 7, 5)
+    load_t.wait()
+    convert(0)
+    relays(1, 0, 1, 2, 3)
+    t_ready(4, 2, 3)
+    relays(1, 4)
+    own_w.wait()
+    compute(0, 0, (0,))
+    compute(0, 1, (0,))
+    compute(1, 1, (0,))
+    relays(2, 0, 1)
     t_ready(5, 6, 7)
-    relays(2, 0, 1, 2)
-    t_ready(4, 2, 3)
+    compute(0, 0, (1,))
+    relays(2, 2)
+    compute(0, 1, (1,))
     relays(2, 3)
-    own_w.wait()
-    compute(0, 0)
+    compute(1, 1, (1,))
+    swapped(2)
     relays(2, 4)
-    compute(0, 1)
-    compute(1, 1)
+    compute(0, 2, (0,))
+    compute(1, 2, (0,))
     relays(3, 0)
-    compute(0, 2)
+    compute(0, 2, (1,))
     relays(3, 1)
-    compute(1, 2)
-    relays(3, 2, 3, 4)
-    compute(0, 3)
-    compute(1, 3)
-    relays(4, 0, 1, 3, 2, 4)
-    compute(0, 4)
+    compute(1, 2, (1,))
+    relays(3, 2, 3)
+    swapped(3)
+    relays(3, 4)
+    compute(0, 3, (0,))
+    compute(1, 3, (0,))
+    compute(0, 3, (1,))
+    relays(4, 0, 1, 3)
+    compute(1, 3, (1,))
+    swapped(4)
+    relays(4, 2, 4)
+    compute(0, 4, (0, 1))
 
     for cp in pending:
         cp.wait_send()
@@ -260,7 +297,7 @@
             pltpu.VMEM((4, 512, 512), bf16),
             pltpu.VMEM((8, 8, 2, 32, 256), f32),
             pltpu.VMEM((2, 32, 128), f32),
-            dma((3,)), dma((8,)), dma((8,)), dma((2, 4, 5)), dma((2, 4, 5)), dma((8, 5)), dma((8, 5)),
+            dma((3,)), dma((8,)), dma((8,)), dma((2, 4, 5)), dma((2, 4, 5)), dma((8, 6)), dma((8, 6)), dma((8,)), dma((8,)),
             dma((8,)), dma((8,)), dma((8, 8)), dma((8, 8)), dma((8,)),
         ],
         compiler_params=pltpu.CompilerParams(

time: 112 us -> 109 us (0.973)
  Pallas kernels: 110 us -> 107 us
    pallas_call x1, Pallas kernels: 110 us -> 107 us  [body(): pl.pallas_call(kernel, out_shape=jax.ShapeDtypeStruct((2, 32, 32, 512), f...]
where the time goes in v4:
time: 109 us
  Pallas kernels  107 us (98%)
  local copies, waits for them, and re-layouts  2.02 us (2%)
    pallas_call x1, Pallas kernels, body(): pl.pallas_call(kernel, out_shape=jax.ShapeDtypeStruct((2, 32, 32, 512), f...  107 us

profile of v4, /device:TPU:1, one launch (start us, length us, event | category | flops | bytes accessed | tf_op | source)
XLA Modules:
  0.0 108.9 jit_solution(16133268213039143234)
XLA Ops:
  0.0 106.8 %shard_map.46 = f32[2,32,32,512]{3,2,1,0:T(8,128)S(1)} custom-call(f32[2,4,32,512]{3,2,1,0:T(8,128)} %t_hbm.1, f32[4,32,2,512]{3,2,1,0:T(2,128)} %w_hbm.1, f32[32]{0:T(128)} %occ.1, f32[1,512]{1,0:T(1,128)} %bitcast.1), custom_call_target="tpu_custom_call" | custom-call | tf_op jit(solution)/shard_map/pallas_call | solution.py:286
  106.8 2.0 %copy.6 = f32[2,32,32,512]{3,2,1,0:T(8,128)} copy(f32[2,32,32,512]{3,2,1,0:T(8,128)S(1)} %shard_map.46) | data formatting | bytes 8388608
